TPU v7x, 32 devices: a whole 2x2x4 slice. The times are simulated.
32 devices in a mesh: req: 4 (over x, core), mlp: 8 (over z, y).
Axes of the slice: x: 2, y: 2, z: 4, core: 2. Of those that a mesh axis runs over, the one named last changes fastest.
Arguments:
- resid: bfloat16 [4096, 3072], P(('req', 'mlp')), may hold values from -6 to 6
- queries: bfloat16 [4096, 1536], P(('req', 'mlp')), may hold values from -240 to 240
- fresh_keys: bfloat16 [4096, 256], P(('req', 'mlp')), may hold values from -6 to 6
- fresh_values: bfloat16 [4096, 256], P(('req', 'mlp')), may hold values from -6 to 6
- paged_key_cache: bfloat16 [64, 128, 256], P(('req', 'mlp')), may hold values from -6 to 6
- paged_value_cache: bfloat16 [64, 128, 256], P(('req', 'mlp')), may hold values from -6 to 6
- page_table: int32 [4, 16], P('req'), may hold values from 0 to 15, as said below
- cache_lengths: int32 [4], P('req'), may hold values from 1 to 2048, as said below
- out_weight: bfloat16 [1536, 3072], replicated, may hold values from -0.15625 to 0.15625
- norm_gain: float32 [3072], replicated, may hold values from 0.5 to 1.5
- gate_weight: bfloat16 [3072, 8192], P('req', 'mlp'), may hold values from -0.109375 to 0.109375
- up_weight: bfloat16 [3072, 8192], P('req', 'mlp'), may hold values from -0.109375 to 0.109375
- down_weight: bfloat16 [8192, 3072], P('mlp', 'req'), may hold values from -0.0625 to 0.0625
Outputs:
- layer_out: bfloat16 [4096, 3072], P(('req', 'mlp'))
Inputs may be any that keep to these rules, and one draw needn't show every extreme that they name: `page_table`: within the 1 request of one index of req the entries are a permutation of 0 to 15. `cache_lengths`: half of the requests hold at most 128 cached tokens, the other half more than 1920; some request holds exactly 2048.
All inputs are finite; a program needn't handle non-finite values.
Results may differ from a plain program's by a relative error of at most 0.0085.
Values may be sent and summed in bfloat16 or wider, within the bound.
A program may use at most 128 MiB of HBM per device.

v0:
```python
import jax
import jax.numpy as jnp
from jax import lax
from jax.sharding import PartitionSpec as P

QUERY_HEADS = 12
KEY_VALUE_HEADS = 2
HEAD_SIZE = 128
REQ_DEV = 1


def body(
    resid,
    queries,
    fresh_keys,
    fresh_values,
    paged_key_cache,
    paged_value_cache,
    page_table,
    cache_lengths,
    out_weight,
    norm_gain,
    gate_weight,
    up_weight,
    down_weight,
):
    token_position = queries.shape[0]
    group_ratio = QUERY_HEADS // KEY_VALUE_HEADS
    scale = HEAD_SIZE ** (-0.5)
    seq_len = token_position * lax.axis_size("mlp") // REQ_DEV
    place = lax.axis_index("mlp")
    first = place * token_position
    request = first // seq_len
    length = lax.dynamic_index_in_dim(cache_lengths, request, 0, keepdims=False)
    table_row = lax.dynamic_index_in_dim(page_table, request, 0, keepdims=False)
    heads_of_queries = queries.reshape(token_position, KEY_VALUE_HEADS, group_ratio, HEAD_SIZE)

    def update(state, joined_keys, joined_values, valid):
        peak, total, summed = state
        heads_of_keys = joined_keys.reshape(-1, KEY_VALUE_HEADS, HEAD_SIZE)
        heads_of_values = joined_values.reshape(-1, KEY_VALUE_HEADS, HEAD_SIZE)
        scores = (
            jnp.einsum(
                "tgrd,kgd->grtk",
                heads_of_queries,
                heads_of_keys,
                preferred_element_type=jnp.float32,
            )
            * scale
        )
        scores = jnp.where(valid, scores, -1e30)
        new_peak = jnp.maximum(peak, jnp.max(scores, axis=-1))
        expo = jnp.where(valid, jnp.exp(scores - new_peak[..., None]), 0.0)
        factor = jnp.exp(peak - new_peak)
        total = total * factor + jnp.sum(expo, axis=-1)
        summed = summed * factor[..., None] + jnp.einsum(
            "grtk,kgd->grtd",
            expo.astype(jnp.bfloat16),
            heads_of_values,
            preferred_element_type=jnp.float32,
        )
        return (new_peak, total, summed)

    state = (
        jnp.full((KEY_VALUE_HEADS, group_ratio, token_position), -1e30, jnp.float32),
        jnp.zeros((KEY_VALUE_HEADS, group_ratio, token_position), jnp.float32),
        jnp.zeros((KEY_VALUE_HEADS, group_ratio, token_position, HEAD_SIZE), jnp.float32),
    )
    rows_of_queries = first + jnp.arange(token_position, dtype=jnp.int32)
    rows_of_keys = lax.all_gather(fresh_keys, "mlp", axis=0, tiled=True)
    rows_of_values = lax.all_gather(fresh_values, "mlp", axis=0, tiled=True)
    count = rows_of_keys.shape[0]
    key_index = jnp.arange(count, dtype=jnp.int32)
    same = key_index[None, :] // seq_len == rows_of_queries[:, None] // seq_len
    valid = same & (key_index[None, :] <= rows_of_queries[:, None])
    state = update(state, rows_of_keys, rows_of_values, valid)
    key_page = lax.all_gather(paged_key_cache, "mlp", axis=0, tiled=True)
    value_page = lax.all_gather(paged_value_cache, "mlp", axis=0, tiled=True)
    count = key_page.shape[0]
    depth = key_page.shape[1]
    cache_positions = jnp.arange(count, dtype=jnp.int32)
    match = table_row[None, :] == cache_positions[:, None]
    owned = jnp.any(match, axis=1)
    page = jnp.sum(
        jnp.where(match, jnp.arange(table_row.shape[0], dtype=jnp.int32)[None, :], 0), axis=1
    )
    positions = page[:, None] * depth + jnp.arange(depth, dtype=jnp.int32)[None, :]
    live = (owned[:, None] & (positions < length)).reshape(1, count * depth)
    joined_keys = key_page.reshape(count * depth, -1)
    joined_values = value_page.reshape(count * depth, -1)
    state = update(state, joined_keys, joined_values, live)
    peak, total, summed = state
    attended = summed / total[..., None]
    attn = (
        jnp.transpose(attended, (2, 0, 1, 3))
        .reshape(token_position, QUERY_HEADS * HEAD_SIZE)
        .astype(jnp.bfloat16)
    )
    h = resid.astype(jnp.float32) + jnp.dot(attn, out_weight, preferred_element_type=jnp.float32)
    normed = (h * lax.rsqrt(jnp.mean(h * h, axis=-1, keepdims=True) + 1e-05) * norm_gain).astype(
        jnp.bfloat16
    )
    whole = lax.all_gather(normed, "mlp", axis=0, tiled=True)

    def add_rows(piece):
        return jnp.dot(whole, piece, preferred_element_type=jnp.float32)

    gate = add_rows(lax.all_gather(gate_weight, "req", axis=0, tiled=True))
    upper = add_rows(lax.all_gather(up_weight, "req", axis=0, tiled=True))
    hidden = (jax.nn.silu(gate) * upper).astype(jnp.bfloat16)
    terms = jnp.dot(
        hidden,
        lax.all_gather(down_weight, "req", axis=1, tiled=True),
        preferred_element_type=jnp.float32,
    )
    mixed = lax.psum_scatter(
        terms.astype(jnp.bfloat16), "mlp", scatter_dimension=0, tiled=True
    ).astype(jnp.float32)
    return (h + mixed).astype(jnp.bfloat16)


def solution(mesh):
    placed = (
        P(("req", "mlp"), None),
        P(("req", "mlp"), None),
        P(("req", "mlp"), None),
        P(("req", "mlp"), None),
        P(("req", "mlp"), None, None),
        P(("req", "mlp"), None, None),
        P("req", None),
        P("req"),
        P(),
        P(),
        P("req", "mlp"),
        P("req", "mlp"),
        P("mlp", "req"),
    )
    return jax.shard_map(
        body, mesh=mesh, in_specs=placed, out_specs=P(("req", "mlp"), None), check_vma=False
    )
```

profile of v0, /device:TPU:0, one launch (start us, length us, event | category | flops | bytes accessed | tf_op | source)
XLA Modules:
  0.0 476.9 jit_solution(3383910963019407040)
XLA Ops:
  6.5 0.7 all-gather.7.cloned.1.call-update
  7.3 0.7 all-gather.9.cloned.1.call-update
  8.1 0.7 all-gather.13.cloned.1.call-update
  9.4 1.2 copy.43
  10.7 1.0 copy.42
  11.6 34.4 %all_gather.25 = bf16[1024,256]{1,0:T(8,128)(2,1)S(1)} all-gather(bf16[128,256]{1,0:T(8,128)(2,1)} %param.16), channel_id=1, replica_groups=mesh['req'=4,'mlp'=8] {'mlp'}, dimensions={0}, use_global_device_ids=true | all-gather | bytes 589824 | tf_op jit(solution)/shard_map/all_gather | solution.py:71
  46.0 1.0 copy.46
  47.0 0.8 fusion.47
  47.8 0.8 select_reduce_fusion
  48.9 28.2 %all_gather.24 = bf16[1024,256]{0,1:T(8,128)(2,1)S(1)} all-gather(bf16[128,256]{0,1:T(8,128)(2,1)S(1)} %copy.42), channel_id=1, replica_groups=mesh['req'=4,'mlp'=8] {'mlp'}, dimensions={0}, use_global_device_ids=true | all-gather | bytes 589824 | tf_op jit(solution)/shard_map/all_gather | solution.py:70
  77.1 3.8 fusion.8
  80.9 1.4 reshape.148
  82.4 14.6 %all-gather.9.cloned.1.call-done = bf16[16,128,256]{2,1,0:T(8,128)(2,1)} async-done(((bf16[2,128,256]{2,1,0:T(8,128)(2,1)}), bf16[16,128,256]{2,1,0:T(8,128)(2,1)}) %all-gather.9.cloned.1.call-update) | async-done | bytes 1048592 | tf_op jit(solution)/shard_map/all_gather | solution.py:78
  97.0 2.4 reshape.149
  99.3 1.9 bitcast_reduce_fusion
  101.5 1.5 fusion.9
  103.1 3.8 fusion.2
  106.9 1.7 fusion.26
  108.6 3.4 fusion.37
  112.1 1.6 multiply_reduce_fusion
  113.6 1.1 multiply_convert_fusion.1
  114.8 0.5 all-gather.15.cloned.1.call-update
  115.4 0.5 all-gather.17.cloned.1.call-update
  116.0 27.7 %all-gather.13.cloned.1.call-done = bf16[3072,1024]{1,0:T(8,128)(2,1)} async-done(((bf16[768,1024]{1,0:T(8,128)(2,1)}), bf16[3072,1024]{1,0:T(8,128)(2,1)}) %all-gather.13.cloned.1.call-update) | async-done | bytes 6291472 | tf_op jit(solution)/shard_map/all_gather | solution.py:108
  143.7 101.1 %all-gather.11.cloned.1.call-done = bf16[1024,3072]{1,0:T(8,128)(2,1)} async-done(((bf16[128,3072]{1,0:T(8,128)(2,1)}), bf16[1024,3072]{1,0:T(8,128)(2,1)}) %all-gather.11.cloned.1.call-update) | async-done | bytes 6291472 | tf_op jit(solution)/shard_map/all_gather | solution.py:103
  244.8 11.9 %fusion.61 = f32[1024,1024]{1,0:T(8,128)} fusion(bf16[1024,3072]{1,0:T(8,128)(2,1)} %all-gather.11.cloned.1.call-done, bf16[3072,1024]{1,0:T(8,128)(2,1)} %all-gather.13.cloned.1.call-done), kind=kOutput, calls=%fused_computation.71 | convolution fusion | flops 6442450944 | bytes 16777216 | tf_op jit(solution)/shard_map/dot_general | solution.py:106
  256.8 34.1 %all-gather.15.cloned.1.call-done = bf16[3072,1024]{1,0:T(8,128)(2,1)} async-done(((bf16[768,1024]{1,0:T(8,128)(2,1)}), bf16[3072,1024]{1,0:T(8,128)(2,1)}) %all-gather.15.cloned.1.call-update) | async-done | bytes 6291472 | tf_op jit(solution)/shard_map/all_gather | solution.py:109
  290.8 12.7 %multiply_convert_fusion = bf16[1024,1024]{1,0:T(8,128)(2,1)} fusion(f32[1024,1024]{1,0:T(8,128)} %fusion.61, bf16[1024,3072]{1,0:T(8,128)(2,1)} %all-gather.11.cloned.1.call-done, bf16[3072,1024]{1,0:T(8,128)(2,1)} %all-gather.15.cloned.1.call-done), kind=kOutput, calls=%fused_computation.16 | convolution fusion | flops 6448742400 | bytes 18874368 | tf_op jit(solution)/shard_map/dot_general | solution.py:106
  303.5 35.1 %all-gather.17.cloned.1.call-done = bf16[1024,3072]{1,0:T(8,128)(2,1)} async-done(((bf16[1024,768]{1,0:T(8,128)(2,1)}), bf16[1024,3072]{1,0:T(8,128)(2,1)}) %all-gather.17.cloned.1.call-update) | async-done | bytes 6291472 | tf_op jit(solution)/shard_map/all_gather | solution.py:113
  338.7 11.1 %convolution_convert_fusion = bf16[1024,3072]{1,0:T(8,128)(2,1)} fusion(bf16[1024,1024]{1,0:T(8,128)(2,1)} %multiply_convert_fusion, bf16[1024,3072]{1,0:T(8,128)(2,1)} %all-gather.17.cloned.1.call-done), kind=kOutput, calls=%fused_computation.12 | convolution fusion | flops 6445596672 | bytes 14680064 | tf_op jit(solution)/shard_map/dot_general | solution.py:111
  349.8 118.1 %reduce-scatter.2.cloned.1.call-done = bf16[128,3072]{1,0:T(8,128)(2,1)} async-done(((bf16[1024,3072]{1,0:T(8,128)(2,1)}), bf16[128,3072]{1,0:T(8,128)(2,1)}) %reduce-scatter.2.cloned.1.call-update) | async-done | bytes 786448 | tf_op jit(solution)/shard_map/reduce_scatter | solution.py:116
  467.8 2.2 add_convert_fusion
  (42 shorter events, 0.9 us)
Async XLA Ops:
  6.5 74.4 %all-gather.7.cloned.1.call-start = ((), (), s32[]{:S(2)}) async-start(), calls=%async_computation.1 | async-start | bytes 1179648 | tf_op jit(solution)/shard_map/all_gather | solution.py:77
  7.3 89.7 %all-gather.9.cloned.1.call-start = ((), (), s32[]{:S(2)}) async-start(), calls=%async_computation.2 | async-start | bytes 1179648 | tf_op jit(solution)/shard_map/all_gather | solution.py:78
  8.0 135.7 %all-gather.13.cloned.1.call-start = ((), (), s32[]{:S(2)}) async-start(), calls=%async_computation.4 | async-start | bytes 7864320 | tf_op jit(solution)/shard_map/all_gather | solution.py:108
  8.7 236.1 %all-gather.11.cloned.1.call-start = ((), (), s32[]{:S(2)}) async-start(), calls=%async_computation.3 | async-start | bytes 7077888 | tf_op jit(solution)/shard_map/all_gather | solution.py:103
  48.9 28.2 %copy-start = (pred[128,1024]{0,1:T(8,128)(4,1)}, pred[128,1024]{0,1:T(8,128)(4,1)S(1)}, u32[]{:S(2)}) copy-start(pred[128,1024]{0,1:T(8,128)(4,1)S(1)} %fusion.42) | copy-start | bytes 393220
  97.0 4.3 slice-start
  99.3 2.2 slice-start.1
  99.3 2.2 copy-start.1
  103.0 3.8 copy-start.4
  106.9 1.7 copy-start.2
  106.9 5.1 %slice-start.2 = ((s8[9437184]{0:T(1024)(128)(4,1)}), s8[4194304]{0:T(1024)(128)(4,1)S(1)}, s32[]{:S(2)}) async-start(s8[9437184]{0:T(1024)(128)(4,1)} %bitcast.105), calls=%async_computation.10 | async-start | bytes 8388608
  108.6 3.4 slice-start.3
  108.6 3.4 slice-start.4
  108.6 3.4 copy-start.3
  112.0 1.6 copy-start.5
  114.8 176.0 %all-gather.15.cloned.1.call-start = ((), (), s32[]{:S(2)}) async-start(), calls=%async_computation.5 | async-start | bytes 7864320 | tf_op jit(solution)/shard_map/all_gather | solution.py:109
  115.4 223.3 %all-gather.17.cloned.1.call-start = ((), (), s32[]{:S(2)}) async-start(), calls=%async_computation.6 | async-start | bytes 7864320 | tf_op jit(solution)/shard_map/all_gather | solution.py:113
  115.9 351.9 %reduce-scatter.2.cloned.1.call-start = ((), (), s32[]{:S(2)}) async-start(), calls=%async_computation.7 | async-start | bytes 7077888 | tf_op jit(solution)/shard_map/reduce_scatter | solution.py:116
Sparse Core Ops, SparseCore 0:
  9.5 44.9 all-gather.6
  56.6 40.3 all-gather.8
  98.5 45.1 all-gather.12
  145.7 99.0 all-gather.10
  246.2 44.5 all-gather.14
  292.2 46.3 all-gather.16
  349.9 117.9 reduce-scatter.1
where the time goes:
time: 477 us
  waiting for transfers between devices  334 us (70%)
  blocking collectives  62.6 us (13%)
  matrix products  48.1 us (10%)
  between operations  14.4 us (3%)
  other arithmetic  10.4 us (2%)
  local copies, waits for them, and re-layouts  7.24 us (2%)
    reduce_scatter x1, waiting for transfers between devices, body(): lax.psum_scatter(terms.astype(jnp.bfloat16), 'mlp', scatter_dimension=0,...  118 us
    all_gather x1, waiting for transfers between devices, body(): whole = lax.all_gather(normed, 'mlp', axis=0, tiled=True)  101 us
    all_gather x1, waiting for transfers between devices, body(): lax.all_gather(down_weight, 'req', axis=1, tiled=True)  35.1 us
    all_gather x1, blocking collectives, body(): rows_of_values = lax.all_gather(fresh_values, 'mlp', axis=0, tiled=True)  34.4 us
    all_gather x1, waiting for transfers between devices, body(): upper = add_rows(lax.all_gather(up_weight, 'req', axis=0, tiled=True))  34.1 us
    all_gather x1, blocking collectives, body(): rows_of_keys = lax.all_gather(fresh_keys, 'mlp', axis=0, tiled=True)  28.2 us
    all_gather x1, waiting for transfers between devices, body(): gate = add_rows(lax.all_gather(gate_weight, 'req', axis=0, tiled=True))  27.7 us
    dot_general x2, matrix products, add_rows(): return jnp.dot(whole, piece, preferred_element_type=jnp.float32)  24.7 us
  transfers between devices with their start and end apart: 7, of which 6 were waited for; matrix products, arithmetic and copies ran while one was open for 11% of the time, Pallas kernels for 0%

commit v1 on v0

--- a/solution.py
+++ b/solution.py
@@ -67,8 +67,13 @@
         jnp.zeros((KEY_VALUE_HEADS, group_ratio, token_position, HEAD_SIZE), jnp.float32),
     )
     rows_of_queries = first + jnp.arange(token_position, dtype=jnp.int32)
-    rows_of_keys = lax.all_gather(fresh_keys, "mlp", axis=0, tiled=True)
-    rows_of_values = lax.all_gather(fresh_values, "mlp", axis=0, tiled=True)
+    rows_of_keys, rows_of_values = jnp.split(
+        lax.all_gather(
+            jnp.concatenate([fresh_keys, fresh_values], axis=1), "mlp", axis=0, tiled=True
+        ),
+        [fresh_keys.shape[1]],
+        axis=1,
+    )
     count = rows_of_keys.shape[0]
     key_index = jnp.arange(count, dtype=jnp.int32)
     same = key_index[None, :] // seq_len == rows_of_queries[:, None] // seq_len

time: 477 us -> 514 us (1.078)
  waiting for transfers between devices: 334 us -> 435 us
  blocking collectives: 62.6 us -> 0 us
    all_gather x2 -> x0, blocking collectives: 62.6 us -> none  [the longest x1 34.4 us: body(): rows_of_values = lax.all_gather(fresh_values, 'mlp', axis=0, tiled=True)]
    all_gather x0 -> x1, waiting for transfers between devices: none -> 39 us  [body(): lax.all_gather(jnp.concatenate([fresh_keys, fresh_values], axis=1), 'mlp'...]
    all_gather x1, waiting for transfers between devices: 0.01 us -> 37.3 us  [body(): key_page = lax.all_gather(paged_key_cache, 'mlp', axis=0, tiled=True)]
    all_gather x1, waiting for transfers between devices: 14.6 us -> 39.7 us  [body(): value_page = lax.all_gather(paged_value_cache, 'mlp', axis=0, tiled=True)]
  transfers between devices with their start and end apart: 7 -> 8, of which waited for: 6 -> 8; matrix products, arithmetic and copies ran while one was open for 11% -> 10% of each run, Pallas kernels for 0% -> 0%
where the time goes in v1:
time: 514 us
  waiting for transfers between devices  435 us (85%)
  matrix products  45.7 us (9%)
  between operations  14.3 us (3%)
  other arithmetic  11.3 us (2%)
  local copies, waits for them, and re-layouts  7.24 us (1%)
    reduce_scatter x1, waiting for transfers between devices, body(): lax.psum_scatter(terms.astype(jnp.bfloat16), 'mlp', scatter_dimension=0,...  118 us
    all_gather x1, waiting for transfers between devices, body(): whole = lax.all_gather(normed, 'mlp', axis=0, tiled=True)  101 us
    all_gather x1, waiting for transfers between devices, body(): value_page = lax.all_gather(paged_value_cache, 'mlp', axis=0, tiled=True)  39.7 us
    all_gather x1, waiting for transfers between devices, body(): lax.all_gather(jnp.concatenate([fresh_keys, fresh_values], axis=1), 'mlp'...  39 us
    all_gather x1, waiting for transfers between devices, body(): key_page = lax.all_gather(paged_key_cache, 'mlp', axis=0, tiled=True)  37.3 us
    all_gather x1, waiting for transfers between devices, body(): lax.all_gather(down_weight, 'req', axis=1, tiled=True)  35.3 us
    all_gather x1, waiting for transfers between devices, body(): upper = add_rows(lax.all_gather(up_weight, 'req', axis=0, tiled=True))  34.1 us
    all_gather x1, waiting for transfers between devices, body(): gate = add_rows(lax.all_gather(gate_weight, 'req', axis=0, tiled=True))  27.5 us
  transfers between devices with their start and end apart: 8, of which 8 were waited for; matrix products, arithmetic and copies ran while one was open for 10% of the time, Pallas kernels for 0%

profile of v1, /device:TPU:0, one launch (start us, length us, event | category | flops | bytes accessed | tf_op | source)
XLA Modules:
  0.0 514.0 jit_solution(13628524094112846392)
XLA Ops:
  6.5 0.7 all-gather.10.cloned.1.call-update
  7.3 0.7 all-gather.12.cloned.1.call-update
  8.1 0.9 copy.43
  9.0 1.0 copy.42
  10.0 0.7 pad_maximum_fusion
  11.3 1.2 copy.44
  13.2 0.8 fusion.47
  14.0 0.8 select_reduce_fusion
  15.1 37.3 %all-gather.10.cloned.1.call-done = bf16[16,128,256]{2,1,0:T(8,128)(2,1)} async-done(((bf16[2,128,256]{2,1,0:T(8,128)(2,1)}), bf16[16,128,256]{2,1,0:T(8,128)(2,1)}) %all-gather.10.cloned.1.call-update) | async-done | bytes 1048592 | tf_op jit(solution)/shard_map/all_gather | solution.py:82
  52.4 1.3 reshape.148
  53.7 39.7 %all-gather.12.cloned.1.call-done = bf16[16,128,256]{2,1,0:T(8,128)(2,1)} async-done(((bf16[2,128,256]{2,1,0:T(8,128)(2,1)}), bf16[16,128,256]{2,1,0:T(8,128)(2,1)}) %all-gather.12.cloned.1.call-update) | async-done | bytes 1048592 | tf_op jit(solution)/shard_map/all_gather | solution.py:83
  93.4 1.3 reshape.149
  94.8 39.0 %all-gather.8.cloned.1.call-done = bf16[1024,512]{0,1:T(8,128)(2,1)} async-done(((bf16[128,512]{0,1:T(8,128)(2,1)}), bf16[1024,512]{0,1:T(8,128)(2,1)}) %all-gather.8.cloned.1.call-update) | async-done | bytes 1048592 | tf_op jit(solution)/shard_map/all_gather | solution.py:71
  133.8 1.3 fusion.61
  135.1 1.1 fusion.8
  136.2 1.9 bitcast_reduce_fusion
  138.2 1.5 fusion.9
  139.7 3.9 fusion.2
  143.7 1.7 fusion.26
  145.4 3.4 fusion.37
  149.0 1.6 multiply_reduce_fusion
  150.5 1.1 multiply_convert_fusion.1
  152.3 0.7 all-gather.20.cloned.1.call-update
  153.1 27.5 %all-gather.16.cloned.1.call-done = bf16[3072,1024]{1,0:T(8,128)(2,1)} async-done(((bf16[768,1024]{1,0:T(8,128)(2,1)}), bf16[3072,1024]{1,0:T(8,128)(2,1)}) %all-gather.16.cloned.1.call-update) | async-done | bytes 6291472 | tf_op jit(solution)/shard_map/all_gather | solution.py:113
  180.5 101.1 %all-gather.14.cloned.1.call-done = bf16[1024,3072]{1,0:T(8,128)(2,1)} async-done(((bf16[128,3072]{1,0:T(8,128)(2,1)}), bf16[1024,3072]{1,0:T(8,128)(2,1)}) %all-gather.14.cloned.1.call-update) | async-done | bytes 6291472 | tf_op jit(solution)/shard_map/all_gather | solution.py:108
  281.6 11.9 %fusion.62 = f32[1024,1024]{1,0:T(8,128)} fusion(bf16[1024,3072]{1,0:T(8,128)(2,1)} %all-gather.14.cloned.1.call-done, bf16[3072,1024]{1,0:T(8,128)(2,1)} %all-gather.16.cloned.1.call-done), kind=kOutput, calls=%fused_computation.73 | convolution fusion | flops 6442450944 | bytes 16777216 | tf_op jit(solution)/shard_map/dot_general | solution.py:111
  293.5 34.1 %all-gather.18.cloned.1.call-done = bf16[3072,1024]{1,0:T(8,128)(2,1)} async-done(((bf16[768,1024]{1,0:T(8,128)(2,1)}), bf16[3072,1024]{1,0:T(8,128)(2,1)}) %all-gather.18.cloned.1.call-update) | async-done | bytes 6291472 | tf_op jit(solution)/shard_map/all_gather | solution.py:114
  327.6 12.7 %multiply_convert_fusion = bf16[1024,1024]{1,0:T(8,128)(2,1)} fusion(f32[1024,1024]{1,0:T(8,128)} %fusion.62, bf16[1024,3072]{1,0:T(8,128)(2,1)} %all-gather.14.cloned.1.call-done, bf16[3072,1024]{1,0:T(8,128)(2,1)} %all-gather.18.cloned.1.call-done), kind=kOutput, calls=%fused_computation.16 | convolution fusion | flops 6448742400 | bytes 18874368 | tf_op jit(solution)/shard_map/dot_general | solution.py:111
  340.3 35.3 %all-gather.20.cloned.1.call-done = bf16[1024,3072]{1,0:T(8,128)(2,1)} async-done(((bf16[1024,768]{1,0:T(8,128)(2,1)}), bf16[1024,3072]{1,0:T(8,128)(2,1)}) %all-gather.20.cloned.1.call-update) | async-done | bytes 6291472 | tf_op jit(solution)/shard_map/all_gather | solution.py:118
  375.6 11.3 %convolution_convert_fusion = bf16[1024,3072]{1,0:T(8,128)(2,1)} fusion(bf16[1024,1024]{1,0:T(8,128)(2,1)} %multiply_convert_fusion, bf16[1024,3072]{1,0:T(8,128)(2,1)} %all-gather.20.cloned.1.call-done), kind=kOutput, calls=%fused_computation.12 | convolution fusion | flops 6445596672 | bytes 14680064 | tf_op jit(solution)/shard_map/dot_general | solution.py:116
  386.9 118.1 %reduce-scatter.2.cloned.1.call-done = bf16[128,3072]{1,0:T(8,128)(2,1)} async-done(((bf16[1024,3072]{1,0:T(8,128)(2,1)}), bf16[128,3072]{1,0:T(8,128)(2,1)}) %reduce-scatter.2.cloned.1.call-update) | async-done | bytes 786448 | tf_op jit(solution)/shard_map/reduce_scatter | solution.py:121
  505.0 2.2 add_convert_fusion
  (32 shorter events, 1.9 us)
Async XLA Ops:
  6.5 45.8 %all-gather.10.cloned.1.call-start = ((), (), s32[]{:S(2)}) async-start(), calls=%async_computation.2 | async-start | bytes 1179648 | tf_op jit(solution)/shard_map/all_gather | solution.py:82
  7.3 86.2 %all-gather.12.cloned.1.call-start = ((), (), s32[]{:S(2)}) async-start(), calls=%async_computation.3 | async-start | bytes 1179648 | tf_op jit(solution)/shard_map/all_gather | solution.py:83
  8.0 125.8 %all-gather.8.cloned.1.call-start = ((), (), s32[]{:S(2)}) async-start(), calls=%async_computation.1 | async-start | bytes 1179648 | tf_op jit(solution)/shard_map/all_gather | solution.py:71
  10.7 169.8 %all-gather.16.cloned.1.call-start = ((), (), s32[]{:S(2)}) async-start(), calls=%async_computation.5 | async-start | bytes 7864320 | tf_op jit(solution)/shard_map/all_gather | solution.py:113
  11.2 270.4 %all-gather.14.cloned.1.call-start = ((), (), s32[]{:S(2)}) async-start(), calls=%async_computation.4 | async-start | bytes 7077888 | tf_op jit(solution)/shard_map/all_gather | solution.py:108
  143.6 5.1 %slice-start = ((s8[9437184]{0:T(1024)(128)(4,1)}), s8[1048576]{0:T(1024)(128)(4,1)S(1)}, s32[]{:S(2)}) async-start(s8[9437184]{0:T(1024)(128)(4,1)} %bitcast.103), calls=%async_computation.9 | async-start | bytes 2097152
  145.4 3.4 slice-start.1
  145.4 3.5 slice-start.2
  145.4 3.6 copy-start
  149.0 1.6 copy-start.1
  151.7 175.9 %all-gather.18.cloned.1.call-start = ((), (), s32[]{:S(2)}) async-start(), calls=%async_computation.6 | async-start | bytes 7864320 | tf_op jit(solution)/shard_map/all_gather | solution.py:114
  152.3 223.3 %all-gather.20.cloned.1.call-start = ((), (), s32[]{:S(2)}) async-start(), calls=%async_computation.7 | async-start | bytes 7864320 | tf_op jit(solution)/shard_map/all_gather | solution.py:118
  153.0 352.0 %reduce-scatter.2.cloned.1.call-start = ((), (), s32[]{:S(2)}) async-start(), calls=%async_computation.8 | async-start | bytes 7077888 | tf_op jit(solution)/shard_map/reduce_scatter | solution.py:121
Sparse Core Ops, SparseCore 0:
  9.5 42.8 all-gather.9
  54.5 38.8 all-gather.11
  95.5 38.2 all-gather.7
  135.2 45.2 all-gather.15
  182.5 99.0 all-gather.13
  283.0 44.5 all-gather.17
  329.2 46.3 all-gather.19
  387.0 117.9 reduce-scatter.1
